TPU v7x, 32 devices: a whole 2x2x4 slice. The times are simulated.
32 devices in a mesh: dp: 8 (over z, x), head: 4 (over y, core).
Axes of the slice: x: 2, y: 2, z: 4, core: 2. Of those that a mesh axis runs over, the one named last changes fastest.
Arguments:
- inputs: bfloat16 [8, 1024, 1152], P('dp', 'head'), may hold values from -6 to 6
- segments: int32 [8, 1024], P('dp'), may hold values from 0 to 7, never falling along the last dimension, each value on 1 to 512 neighbouring positions
- cotangent: bfloat16 [8, 1024, 1152], P('dp', 'head'), may hold values from -6 to 6
- query_weight: bfloat16 [1152, 1024], replicated, may hold values from -0.1875 to 0.1875
- key_weight: bfloat16 [1152, 256], replicated, may hold values from -0.1875 to 0.1875
- value_weight: bfloat16 [1152, 256], replicated, may hold values from -0.1875 to 0.1875
- out_weight: bfloat16 [1024, 1152], replicated, may hold values from -0.1875 to 0.1875
- gate_weight: bfloat16 [1152, 6912], P(None, 'head'), may hold values from -0.1875 to 0.1875
- up_weight: bfloat16 [1152, 6912], P(None, 'head'), may hold values from -0.1875 to 0.1875
- down_weight: bfloat16 [6912, 1152], P('head'), may hold values from -0.078125 to 0.078125
- input_gain: float32 [1152], replicated, may hold values from 0.1 to 1.9
- query_gain: float32 [256], replicated, may hold values from 0.1 to 1.9
- key_gain: float32 [256], replicated, may hold values from 0.1 to 1.9
- attn_gain: float32 [1152], replicated, may hold values from 0.1 to 1.9
- pre_ff_gain: float32 [1152], replicated, may hold values from 0.1 to 1.9
- post_ff_gain: float32 [1152], replicated, may hold values from 0.1 to 1.9
Outputs:
- layer_output: bfloat16 [8, 1024, 1152], P('dp', 'head')
- input_grad: float32 [8, 1024, 1152], P('dp', 'head')
- query_weight_grad: float32 [1152, 1024], replicated
- key_weight_grad: float32 [1152, 256], replicated
- value_weight_grad: float32 [1152, 256], replicated
- out_weight_grad: float32 [1024, 1152], replicated
- gate_weight_grad: float32 [1152, 6912], P('dp', 'head')
- up_weight_grad: float32 [1152, 6912], P('dp', 'head')
- down_weight_grad: float32 [6912, 1152], P('head', 'dp')
- input_gain_grad: float32 [1152], replicated
- query_gain_grad: float32 [256], replicated
- key_gain_grad: float32 [256], replicated
- attn_gain_grad: float32 [1152], replicated
- pre_ff_gain_grad: float32 [1152], replicated
- post_ff_gain_grad: float32 [1152], replicated
Inputs may be any that keep to these rules, and one draw needn't show every extreme that they name: `segments`: within a row the document numbers never fall; each of the 8 documents has 1 to 512 tokens, and one has exactly 512.
All inputs are finite; a program needn't handle non-finite values.
Results may differ from a plain program's by a relative error of at most 0.02.
Values may be sent and summed in bfloat16 or wider, within the bound.
No kernel may reach another device: no remote copies, remote signals or barrier semaphores. Data moves between devices by JAX's collectives and lax.ppermute only.
A program may use at most 192 MiB of HBM per device.

v0:
```python
from functools import partial

import jax
import jax.numpy as jnp
from jax import lax
from jax.sharding import PartitionSpec as P

EPSILON = 1e-06
ROPE_BASE = 1000000.0
MASKED = -1e30


def for_sending(x):
    return jax.tree.map(lambda a: a.astype(jnp.bfloat16) if a.dtype == jnp.float32 else a, x)


def rms_norm(values, gain):
    return values * lax.rsqrt(jnp.mean(values * values, axis=-1, keepdims=True) + EPSILON) * gain


def positions_of(segment_ids):
    count = segment_ids.shape[0]
    position_index = jnp.arange(count, dtype=jnp.int32)
    previous = jnp.concatenate([segment_ids[:1] - 1, segment_ids[:-1]])
    starts = jnp.where(segment_ids != previous, position_index, 0)
    return position_index - lax.cummax(starts, axis=0)


def rotary(values, positions, sign):
    half_width = values.shape[-1] // 2
    frequency = ROPE_BASE ** (-2.0 * jnp.arange(half_width, dtype=jnp.float32) / values.shape[-1])
    angle = positions.astype(jnp.float32)[:, None] * frequency[None, :]
    cosine_part = jnp.cos(angle)
    sine_part = jnp.sin(angle) * sign
    if values.ndim == 3:
        cosine_part = cosine_part[:, None, :]
        sine_part = sine_part[:, None, :]
    leading = values[..., :half_width]
    trailing = values[..., half_width:]
    return jnp.concatenate(
        [
            leading * cosine_part - trailing * sine_part,
            trailing * cosine_part + leading * sine_part,
        ],
        axis=-1,
    )


def product(left, right):
    return jnp.dot(left, right, preferred_element_type=jnp.float32)


def product_tn(left, right):
    return lax.dot_general(
        left, right, (((0,), (0,)), ((), ())), preferred_element_type=jnp.float32
    )


def product_nt(left, right):
    return lax.dot_general(
        left, right, (((1,), (1,)), ((), ())), preferred_element_type=jnp.float32
    )


def shards(
    inputs,
    segments,
    cotangent,
    query_weight,
    key_weight,
    value_weight,
    out_weight,
    gate_weight,
    up_weight,
    down_weight,
    input_gain,
    query_gain,
    key_gain,
    attn_gain,
    pre_ff_gain,
    post_ff_gain,
):
    low_type = jnp.bfloat16
    tok_rows = inputs.shape[1]
    head_dim = key_weight.shape[1]
    query_heads = query_weight.shape[1] // head_dim
    seq_len = segments.shape[1]
    block_rows = min(512, seq_len)
    score_scale = head_dim ** (-0.5)
    gelu_tanh = partial(jax.nn.gelu, approximate=True)
    x_rows = inputs[0].astype(jnp.float32)
    segment_ids = segments[0]
    all_positions = positions_of(segment_ids)
    own_start = lax.axis_index("head") * tok_rows
    positions = lax.dynamic_slice_in_dim(all_positions, own_start, tok_rows)
    position_index = jnp.arange(seq_len, dtype=jnp.int32)
    normed, input_pull = jax.vjp(rms_norm, x_rows, input_gain)
    normed_low = normed.astype(low_type)
    q_proj = product(normed_low, query_weight).reshape(tok_rows, query_heads, head_dim)
    k_proj = product(normed_low, key_weight)
    v_low = product(normed_low, value_weight).astype(low_type)
    q_normed, query_pull = jax.vjp(rms_norm, q_proj, query_gain)
    k_normed, key_pull = jax.vjp(rms_norm, k_proj, key_gain)
    q_low = rotary(q_normed, positions, 1.0).astype(low_type)
    k_low = rotary(k_normed, positions, 1.0).astype(low_type)
    query_rows = lax.all_to_all(q_low, "head", split_axis=1, concat_axis=0, tiled=True)[:, 0, :]
    row_segments_all = jnp.take(segment_ids, position_index)
    key_rows, value_rows = (
        lax.all_gather(k_low, "head", axis=0, tiled=True),
        lax.all_gather(v_low, "head", axis=0, tiled=True),
    )

    def masked_scores(start_row):
        row_slice = query_rows[start_row : start_row + block_rows]
        raw_scores = product_nt(row_slice, key_rows) * score_scale
        row_ids = position_index[start_row : start_row + block_rows]
        row_segments = row_segments_all[start_row : start_row + block_rows]
        allowed = (row_segments[:, None] == segment_ids[None, :]) & (
            position_index[None, :] <= row_ids[:, None]
        )
        return jnp.where(allowed, raw_scores, MASKED)

    attended_blocks = []
    log_blocks = []
    for start_row in range(0, seq_len, block_rows):
        masked = masked_scores(start_row)
        row_max = jnp.max(masked, axis=1, keepdims=True)
        exponent = jnp.exp(masked - row_max)
        row_total = jnp.sum(exponent, axis=1, keepdims=True)
        probabilities = (exponent / row_total).astype(low_type)
        attended_blocks.append(product(probabilities, value_rows))
        log_blocks.append(row_max + jnp.log(row_total))
    attended_low = jnp.concatenate(attended_blocks, axis=0).astype(low_type)
    log_totals = jnp.concatenate(log_blocks, axis=0)
    mixed_rows = lax.all_to_all(
        attended_low[:, None, :], "head", split_axis=0, concat_axis=1, tiled=True
    )
    mixed_rows = mixed_rows.reshape(tok_rows, query_heads * head_dim)
    projected = product(mixed_rows, out_weight)
    attn_branch, attn_pull = jax.vjp(rms_norm, projected, attn_gain)
    after_attn = x_rows + attn_branch
    pre_normed, pre_pull = jax.vjp(rms_norm, after_attn, pre_ff_gain)
    rows_all = lax.all_gather(pre_normed.astype(low_type), "head", axis=0, tiled=True)
    gate_act = product(rows_all, gate_weight)
    up_act = product(rows_all, up_weight)
    gelu_gate, gelu_pull = jax.vjp(gelu_tanh, gate_act)
    hidden_low = (gelu_gate * up_act).astype(low_type)
    ff_out = lax.psum_scatter(
        product(
            lax.slice_in_dim(hidden_low, 0, tok_rows * lax.axis_size("head"), axis=0), down_weight
        ).astype(jnp.bfloat16),
        "head",
        scatter_dimension=0,
        tiled=True,
    ).astype(jnp.float32)
    post_branch, post_pull = jax.vjp(rms_norm, ff_out, post_ff_gain)
    layer_out = after_attn + post_branch
    out_grad = cotangent[0].astype(jnp.float32)
    ff_grad, post_gain_grad = post_pull(out_grad)
    ff_grad_all = lax.all_gather(for_sending(ff_grad.astype(low_type)), "head", axis=0, tiled=True)
    down_grad = product_tn(hidden_low, ff_grad_all)
    hidden_grad = product_nt(ff_grad_all, down_weight)
    up_grad_low = (hidden_grad * gelu_gate).astype(low_type)
    gate_grad_low = gelu_pull(hidden_grad * up_act)[0].astype(low_type)
    gate_grad = product_tn(rows_all, gate_grad_low)
    up_grad = product_tn(rows_all, up_grad_low)
    up_slice = lax.slice_in_dim(up_grad_low, 0, tok_rows * lax.axis_size("head"), axis=0)
    pre_grad = lax.psum_scatter(
        (product_nt(gate_grad_low, gate_weight) + product_nt(up_slice, up_weight)).astype(
            jnp.bfloat16
        ),
        "head",
        scatter_dimension=0,
        tiled=True,
    ).astype(jnp.float32)
    after_from_ff, pre_gain_grad = pre_pull(pre_grad)
    after_grad = out_grad + after_from_ff
    projected_grad, attn_gain_grad = attn_pull(after_grad)
    projected_low = projected_grad.astype(low_type)
    out_weight_grad = product_tn(mixed_rows, projected_low)
    mixed_grad = product_nt(projected_low, out_weight).astype(low_type)
    mixed_grad = mixed_grad.reshape(tok_rows, query_heads, head_dim)
    attended_grad = lax.all_to_all(mixed_grad, "head", split_axis=1, concat_axis=0, tiled=True)[
        :, 0, :
    ]
    query_blocks = []
    key_grad = jnp.zeros((seq_len, head_dim), jnp.float32)
    value_grad = jnp.zeros((seq_len, head_dim), jnp.float32)
    for start_row in range(0, seq_len, block_rows):
        masked = masked_scores(start_row)
        probabilities = jnp.exp(masked - log_totals[start_row : start_row + block_rows])
        grad_rows = attended_grad[start_row : start_row + block_rows]
        value_grad = value_grad + product_tn(probabilities.astype(low_type), grad_rows)
        prob_grad = product_nt(grad_rows, value_rows)
        row_delta = jnp.sum(prob_grad * probabilities, axis=1, keepdims=True)
        score_grad = (probabilities * (prob_grad - row_delta)).astype(low_type)
        query_blocks.append(product(score_grad, key_rows) * score_scale)
        key_grad = (
            key_grad
            + product_tn(score_grad, query_rows[start_row : start_row + block_rows]) * score_scale
        )
    query_grad_low = jnp.concatenate(query_blocks, axis=0).astype(low_type)
    query_back = lax.all_to_all(
        query_grad_low[:, None, :], "head", split_axis=0, concat_axis=1, tiled=True
    )
    key_share, value_share = (
        lax.psum_scatter(
            key_grad.astype(jnp.bfloat16), "head", scatter_dimension=0, tiled=True
        ).astype(jnp.float32),
        lax.psum_scatter(
            value_grad.astype(jnp.bfloat16), "head", scatter_dimension=0, tiled=True
        ).astype(jnp.float32),
    )
    q_proj_grad, query_gain_grad = query_pull(
        rotary(query_back.astype(jnp.float32), positions, -1.0)
    )
    key_back = key_share.astype(low_type).astype(jnp.float32)
    k_proj_grad, key_gain_grad = key_pull(rotary(key_back, positions, -1.0))
    q_grad_low = q_proj_grad.reshape(tok_rows, query_heads * head_dim).astype(low_type)
    k_grad_low = k_proj_grad.astype(low_type)
    v_grad_low = value_share.astype(low_type)
    query_weight_grad = product_tn(normed_low, q_grad_low)
    key_weight_grad = product_tn(normed_low, k_grad_low)
    value_weight_grad = product_tn(normed_low, v_grad_low)
    normed_grad = (
        product_nt(q_grad_low, query_weight)
        + product_nt(k_grad_low, key_weight)
        + product_nt(v_grad_low, value_weight)
    )
    input_from_norm, input_gain_grad = input_pull(normed_grad)
    input_grad = after_grad + input_from_norm
    summed = lax.psum(
        (
            query_weight_grad,
            key_weight_grad,
            value_weight_grad,
            out_weight_grad,
            input_gain_grad,
            query_gain_grad,
            key_gain_grad,
            attn_gain_grad,
            pre_gain_grad,
            post_gain_grad,
        ),
        ("dp", "head"),
    )
    gate_share, up_share, down_share = (
        lax.psum_scatter(
            gate_grad.astype(jnp.bfloat16), "dp", scatter_dimension=0, tiled=True
        ).astype(jnp.float32),
        lax.psum_scatter(
            up_grad.astype(jnp.bfloat16), "dp", scatter_dimension=0, tiled=True
        ).astype(jnp.float32),
        lax.psum_scatter(
            down_grad.astype(jnp.bfloat16), "dp", scatter_dimension=1, tiled=True
        ).astype(jnp.float32),
    )
    return (
        layer_out.astype(low_type)[None],
        input_grad[None],
        summed[0],
        summed[1],
        summed[2],
        summed[3],
        gate_share,
        up_share,
        down_share,
        summed[4],
        summed[5],
        summed[6],
        summed[7],
        summed[8],
        summed[9],
    )


def solution(mesh):
    in_specs = (
        P("dp", "head", None),
        P("dp", None),
        P("dp", "head", None),
        P(),
        P(),
        P(),
        P(),
        P(None, "head"),
        P(None, "head"),
        P("head", None),
        P(),
        P(),
        P(),
        P(),
        P(),
        P(),
    )
    out_specs = (
        P("dp", "head", None),
        P("dp", "head", None),
        P(),
        P(),
        P(),
        P(),
        P("dp", "head"),
        P("dp", "head"),
        P("head", "dp"),
        P(),
        P(),
        P(),
        P(),
        P(),
        P(),
    )
    return jax.shard_map(shards, mesh=mesh, in_specs=in_specs, out_specs=out_specs, check_vma=False)
```

profile of v0, /device:TPU:0, one launch (start us, length us, event | category | flops | bytes accessed | tf_op | source)
XLA Modules:
  0.0 872.3 jit_solution(2436494161311775190)
XLA Ops:
  13.7 4.4 copy.65
  18.1 3.6 multiply_reduce_fusion.8
  25.6 4.3 all-to-all-start
  30.5 9.1 %gather_fusion = s32[1024]{0:T(1024)} fusion(s32[1024]{0:T(1024)S(1)} %bitcast.161, s32[1024]{0:T(1024)} %iota_clamp_fusion), kind=kCustom, calls=%fused_computation | custom fusion | bytes 12288 | tf_op jit(solution)/shard_map/jit(_take)/gather | solution.py:107
  43.4 9.0 %all_gather.12 = bf16[1024,256]{0,1:T(8,128)(2,1)} all-gather(bf16[256,256]{0,1:T(8,128)(2,1)S(1)} %pad_maximum_fusion.5), channel_id=1, replica_groups=mesh['dp'=8,'head'=4] {'head'}, dimensions={0}, use_global_device_ids=true | all-gather | bytes 655360 | tf_op jit(solution)/shard_map/all_gather | solution.py:109
  52.5 7.3 all_gather.13
  59.7 2.0 fusion.94
  61.8 1.8 copy.53
  63.6 1.8 copy.54
  65.4 1.9 fusion.96
  73.3 2.0 reshape.403
  75.3 12.3 %all_to_all.54 = bf16[4,2,32768]{2,1,0:T(2,128)(2,1)S(1)} all-to-all(bf16[4,2,32768]{2,1,0:T(2,128)(2,1)} %reshape.403), channel_id=1, replica_groups=mesh['dp'=8,'head'=4] {'head'}, dimensions={0} | all-to-all | bytes 1048576 | tf_op jit(solution)/shard_map/all_to_all | solution.py:135
  89.3 2.1 copy.66
  97.6 24.4 %all-gather.3.cloned.1.call-done = bf16[1024,1152]{1,0:T(8,128)(2,1)} async-done(((bf16[256,1152]{1,0:T(8,128)(2,1)}), bf16[1024,1152]{1,0:T(8,128)(2,1)}) %all-gather.3.cloned.1.call-update) | async-done | bytes 2359312 | tf_op jit(solution)/shard_map/all_gather | solution.py:143
  122.0 7.4 fusion.98
  129.5 7.9 multiply_convert_fusion.1
  139.1 6.3 convolution_convert_fusion.3
  145.5 32.9 %reduce-scatter.8.cloned.1.call-done = bf16[256,1152]{1,0:T(8,128)(2,1)} async-done(((bf16[1024,1152]{1,0:T(8,128)(2,1)}), bf16[256,1152]{1,0:T(8,128)(2,1)}) %reduce-scatter.8.cloned.1.call-update) | async-done | bytes 589840 | tf_op jit(solution)/shard_map/reduce_scatter | solution.py:148
  179.8 2.4 fusion.43
  182.2 2.2 fusion.39
  184.7 24.0 %all-gather.5.cloned.1.call-done = bf16[1024,1152]{1,0:T(8,128)(2,1)} async-done(((bf16[256,1152]{1,0:T(8,128)(2,1)}), bf16[1024,1152]{1,0:T(8,128)(2,1)}) %all-gather.5.cloned.1.call-update) | async-done | bytes 2359312 | tf_op jit(solution)/shard_map/all_gather | solution.py:160
  208.6 14.8 %multiply_convert_fusion = (bf16[1024,1728]{0,1:T(8,128)(2,1)S(1)}, bf16[1024,1728]{0,1:T(8,128)(2,1)S(1)}) fusion(f32[1024,1728]{0,1:T(8,128)} %copy-done.94, f32[1024,1728]{0,1:T(8,128)} %get-tuple-element.71, bf16[1024,1152]{1,0:T(8,128)(2,1)} %all-gather.5.cloned.1.call-done, bf16[1728,1152]{1,0:T(8,128)(2,1)} %param.25), kind=kOutput, calls=%fused_computation.13 | convolution fusion | flops 4119330816 | bytes 27574272 | tf_op jit(solution)/shard_map/dot_general | solution.py:60
  223.5 5.2 fusion.99
  228.7 6.6 add_convert_fusion
  235.4 33.0 %reduce-scatter.10.cloned.1.call-done = bf16[256,1152]{1,0:T(8,128)(2,1)} async-done(((bf16[1024,1152]{1,0:T(8,128)(2,1)}), bf16[256,1152]{1,0:T(8,128)(2,1)}) %reduce-scatter.10.cloned.1.call-update) | async-done | bytes 589840 | tf_op jit(solution)/shard_map/reduce_scatter | solution.py:168
  268.4 2.5 fusion.34
  271.6 3.9 multiply_reduce_fusion.2
  277.6 4.3 all-to-all-start.2
  282.0 8.8 %all-to-all-done.2 = bf16[256,4,256]{2,0,1:T(8,128)(2,1)} async-done(((bf16[256,4,256]{2,0,1:T(8,128)(2,1)}), bf16[256,4,256]{2,0,1:T(8,128)(2,1)}, u32[]{:S(2)}, u32[]{:S(2)}) %all-to-all-start.2) | async-done | bytes 524320 | tf_op jit(solution)/shard_map/all_to_all | solution.py:183
  298.9 2.2 fusion.52
  302.6 9.4 %convolution_convert_fusion = bf16[1728,1152]{0,1:T(8,128)(2,1)} fusion(bf16[1024,1728]{0,1:T(8,128)(2,1)} %copy-done.93, bf16[1024,1152]{1,0:T(8,128)(2,1)} %all-gather.5.cloned.1.call-done), kind=kOutput, calls=%fused_computation.3 | convolution fusion | flops 4078854144 | bytes 9879552 | tf_op jit(solution)/shard_map/dot_general | solution.py:54
  313.7 8.5 convolution_convert_fusion.1
  322.3 8.2 convolution_convert_fusion.2
  334.8 3.5 all-to-all-start.3
  338.3 3.0 fusion.102
  341.4 7.9 all-to-all-done.3
  356.9 2.4 fusion.85
  359.4 3.1 fusion.59
  367.1 42.1 %all-reduce = (f32[1152]{0:T(1024)}, f32[256]{0:T(256)}, f32[256]{0:T(256)}, f32[1152]{0:T(1024)}, f32[1152]{0:T(1024)}, /*index=5*/f32[1152]{0:T(1024)}) all-reduce(f32[1152]{0:T(1024)S(1)} %get-tuple-element.21, f32[256]{0:T(256)S(1)} %get-tuple-element.17, ...), channel_id=1, replica_groups=mesh['dp'=8,'head'=4] {'dp','head'}, use_global_device_ids=true, to_apply=%region_32.33 | all-reduce | flops 5120 | bytes 40960 | tf_op jit(solution)/shard_map/psum | solution.py:232
  410.6 29.6 %reduce-scatter.20.cloned.1.call-done = bf16[1728,144]{0,1:T(8,128)(2,1)} async-done(((bf16[1728,1152]{0,1:T(8,128)(2,1)}), bf16[1728,144]{0,1:T(8,128)(2,1)}) %reduce-scatter.20.cloned.1.call-update) | async-done | bytes 497680 | tf_op jit(solution)/shard_map/reduce_scatter | solution.py:254
  440.2 2.1 convert_element_type.202
  442.3 89.1 %reduce-scatter.18.cloned.1.call-done = bf16[144,1728]{1,0:T(8,128)(2,1)} async-done(((bf16[1152,1728]{1,0:T(8,128)(2,1)}), bf16[144,1728]{1,0:T(8,128)(2,1)}) %reduce-scatter.18.cloned.1.call-update) | async-done | bytes 497680 | tf_op jit(solution)/shard_map/reduce_scatter | solution.py:251
  531.3 2.1 convert_element_type.200
  533.4 89.1 %reduce-scatter.16.cloned.1.call-done = bf16[144,1728]{1,0:T(8,128)(2,1)} async-done(((bf16[1152,1728]{1,0:T(8,128)(2,1)}), bf16[144,1728]{1,0:T(8,128)(2,1)}) %reduce-scatter.16.cloned.1.call-update) | async-done | bytes 497680 | tf_op jit(solution)/shard_map/reduce_scatter | solution.py:248
  622.5 2.1 convert_element_type.198
  624.6 229.0 %all-reduce.4.cloned.1.call-done = (f32[1152,1024]{1,0:T(8,128)}, f32[1152,256]{1,0:T(8,128)}, f32[1152,256]{1,0:T(8,128)}, f32[1024,1152]{1,0:T(8,128)}) async-done(((f32[1152,1024]{1,0:T(8,128)}, f32[1152,256]{1,0:T(8,128)}, f32[1152,256]{1,0:T(8,128)}, f32[1024,1152]{1,0:T(8,128)}), (f32[1152,1024]{1,0:T(8,128)}, f32[1152,256]{1,0:T(8,128)}, f32[1152,256]{1,0:T(8,128)}, ...) | async-done | bytes 11796496 | tf_op jit(solution)/shard_map/psum | solution.py:232
  853.6 5.4 copy.76
  861.7 2.4 copy.79
  (306 shorter events, 66.8 us)
Async XLA Ops:
  7.2 85.5 %copy-start = (bf16[1024,1152]{1,0:T(8,128)(2,1)S(1)}, bf16[1024,1152]{1,0:T(8,128)(2,1)}, u32[]{:S(2)}) copy-start(bf16[1024,1152]{1,0:T(8,128)(2,1)} %param.22) | copy-start | bytes 7077892
  7.2 14.8 %copy-start.84 = (f32[128]{0:T(128)}, f32[128]{0:T(128)S(1)}, u32[]{:S(2)}) copy-start(f32[128]{0:T(128)S(1)} %multiply_power_fusion) | copy-start | bytes 1540
  9.8 8.3 copy-start.50
  13.7 4.4 copy-start.80
  13.7 8.2 copy-start.27
  13.7 8.1 copy-start.55
  13.7 4.4 copy-start.3
  18.1 5.1 copy-start.61
  24.6 5.9 copy-start.2
  25.6 34.1 %all-to-all-start = ((bf16[256,4,256]{0,2,1:T(8,128)(2,1)}), bf16[256,4,256]{0,2,1:T(8,128)(2,1)}, u32[]{:S(2)}, u32[]{:S(2)}) async-start(bf16[256,4,256]{0,2,1:T(8,128)(2,1)} %pad_maximum_fusion.1), calls=%async_computation | async-start | bytes 1048576 | tf_op jit(solution)/shard_map/all_to_all | solution.py:106
  29.9 92.1 %all-gather.3.cloned.1.call-start = ((), (), s32[]{:S(2)}) async-start(), calls=%async_computation.11 | async-start | bytes 2949120 | tf_op jit(solution)/shard_map/all_gather | solution.py:143
  30.5 10.9 %copy-start.40 = (bf16[1152,256]{1,0:T(8,128)(2,1)S(1)}, bf16[1152,256]{1,0:T(8,128)(2,1)}, u32[]{:S(2)}) copy-start(bf16[1152,256]{1,0:T(8,128)(2,1)} %param.21) | copy-start | bytes 1769476
  42.5 22.9 %copy-start.83 = (s32[512]{0:T(512)S(1)}, s32[512]{0:T(512)}, u32[]{:S(2)}) copy-start(s32[512]{0:T(512)} %slice.99) | copy-start | bytes 6148
  59.7 10.6 %copy-start.19 = (bf16[1024,256]{1,0:T(8,128)(2,1)}, bf16[1024,256]{1,0:T(8,128)(2,1)S(1)}, u32[]{:S(2)}) copy-start(bf16[1024,256]{1,0:T(8,128)(2,1)S(1)} %all_gather.13) | copy-start | bytes 1572868
  95.1 34.4 %copy-start.63 = (f32[256]{0:T(256)}, f32[256]{0:T(256)S(1)}, u32[]{:S(2)}) copy-start(f32[256]{0:T(256)S(1)} %get-tuple-element.38) | copy-start | bytes 3076
  95.1 34.3 %copy-start.59 = (f32[256]{0:T(256)}, f32[256]{0:T(256)S(1)}, u32[]{:S(2)}) copy-start(f32[256]{0:T(256)S(1)} %fusion.83) | copy-start | bytes 3076
  97.1 81.4 %reduce-scatter.8.cloned.1.call-start = ((), (), s32[]{:S(2)}) async-start(), calls=%async_computation.12 | async-start | bytes 2949120 | tf_op jit(solution)/shard_map/reduce_scatter | solution.py:148
  122.0 7.4 copy-start.88
  122.0 7.4 copy-start.90
  129.5 7.9 copy-start.94
  129.5 9.6 %copy-start.86 = (bf16[1728,1152]{1,0:T(8,128)(2,1)S(1)}, bf16[1728,1152]{1,0:T(8,128)(2,1)}, u32[]{:S(2)}) copy-start(bf16[1728,1152]{1,0:T(8,128)(2,1)} %param.25) | copy-start | bytes 11943940
  145.5 63.1 %all-gather.5.cloned.1.call-start = ((), (), s32[]{:S(2)}) async-start(), calls=%async_computation.13 | async-start | bytes 2949120 | tf_op jit(solution)/shard_map/all_gather | solution.py:160
  184.4 83.9 %reduce-scatter.10.cloned.1.call-start = ((), (), s32[]{:S(2)}) async-start(), calls=%async_computation.14 | async-start | bytes 2949120 | tf_op jit(solution)/shard_map/reduce_scatter | solution.py:168
  208.6 14.9 %copy-start.87 = (bf16[1152,1728]{0,1:T(8,128)(2,1)S(1)}, bf16[1152,1728]{0,1:T(8,128)(2,1)}, u32[]{:S(2)}) copy-start(bf16[1152,1728]{0,1:T(8,128)(2,1)} %param.23) | copy-start | bytes 11943940
  223.5 5.2 copy-start.92
  223.5 5.2 copy-start.95
  223.5 5.2 copy-start.89
  275.8 6.1 copy-start.73
  275.8 6.1 copy-start.75
  275.8 6.1 copy-start.77
  275.8 6.1 copy-start.79
  276.7 15.1 %copy-start.7 = (f32[512,1024]{1,0:T(8,128)S(1)}, f32[512,1024]{1,0:T(8,128)}, u32[]{:S(2)}) copy-start(f32[512,1024]{1,0:T(8,128)} %copy-done.6) | copy-start | bytes 6291460
  276.7 15.1 %copy-start.20 = (bf16[1024,256]{1,0:T(8,128)(2,1)S(1)}, bf16[1024,256]{1,0:T(8,128)(2,1)}, u32[]{:S(2)}) copy-start(bf16[1024,256]{1,0:T(8,128)(2,1)} %copy-done.19) | copy-start | bytes 1572868
  277.6 13.2 %all-to-all-start.2 = ((bf16[256,4,256]{2,0,1:T(8,128)(2,1)}), bf16[256,4,256]{2,0,1:T(8,128)(2,1)}, u32[]{:S(2)}, u32[]{:S(2)}) async-start(bf16[256,4,256]{2,0,1:T(8,128)(2,1)} %bitcast.179), calls=%async_computation.4 | async-start | bytes 1048576 | tf_op jit(solution)/shard_map/all_to_all | solution.py:183
  281.9 69.3 %reduce-scatter.12.cloned.1.call-start = ((), (), s32[]{:S(2)}) async-start(), calls=%async_computation.15 | async-start | bytes 655360 | tf_op jit(solution)/shard_map/reduce_scatter | solution.py:207
  298.8 58.1 %reduce-scatter.14.cloned.1.call-start = ((), (), s32[]{:S(2)}) async-start(), calls=%async_computation.16 | async-start | bytes 655360 | tf_op jit(solution)/shard_map/reduce_scatter | solution.py:210
  302.6 137.6 %reduce-scatter.20.cloned.1.call-start = ((), (), s32[]{:S(2)}) async-start(), calls=%async_computation.19 | async-start | bytes 4644864 | tf_op jit(solution)/shard_map/reduce_scatter | solution.py:254
  312.0 219.3 %reduce-scatter.18.cloned.1.call-start = ((), (), s32[]{:S(2)}) async-start(), calls=%async_computation.18 | async-start | bytes 4644864 | tf_op jit(solution)/shard_map/reduce_scatter | solution.py:251
  322.2 300.3 %reduce-scatter.16.cloned.1.call-start = ((), (), s32[]{:S(2)}) async-start(), calls=%async_computation.17 | async-start | bytes 4644864 | tf_op jit(solution)/shard_map/reduce_scatter | solution.py:248
  332.8 5.5 copy-start.17
  332.8 5.5 copy-start.26
  334.8 14.5 %all-to-all-start.3 = ((bf16[4,2,32768]{2,1,0:T(2,128)(2,1)}), bf16[4,2,32768]{2,1,0:T(2,128)(2,1)S(1)}, u32[]{:S(2)}, u32[]{:S(2)}) async-start(bf16[4,2,32768]{2,1,0:T(2,128)(2,1)} %reshape.405), calls=%async_computation.5 | async-start | bytes 1048576 | tf_op jit(solution)/shard_map/all_to_all | solution.py:203
  338.3 515.3 %all-reduce.4.cloned.1.call-start = ((), (), s32[]{:S(2)}) async-start(), calls=%async_computation.20 | async-start | bytes 23592960 | tf_op jit(solution)/shard_map/psum | solution.py:232
  366.4 42.8 %copy-start.69 = (f32[256]{0:T(256)S(1)}, f32[256]{0:T(256)}, u32[]{:S(2)}) copy-start(f32[256]{0:T(256)} %copy-done.68) | copy-start | bytes 3076
  366.4 42.8 %copy-start.12 = (f32[256,1152]{1,0:T(8,128)S(1)}, f32[256,1152]{1,0:T(8,128)}, u32[]{:S(2)}) copy-start(f32[256,1152]{1,0:T(8,128)} %copy-done.11) | copy-start | bytes 3538948
  853.6 8.1 slice-start
  853.6 5.4 copy-start.36
  853.6 8.1 slice-start.1
  (63 other events, 122.1 us)
Sparse Core Ops, SparseCore 0:
  97.2 24.7 all-gather.2
  145.6 32.8 reduce-scatter.7
  184.6 24.0 all-gather.4
  235.5 32.8 reduce-scatter.9
  298.9 21.6 reduce-scatter.11
  323.0 24.2 reduce-scatter.13
  350.8 89.3 reduce-scatter.19
  443.8 87.5 reduce-scatter.17
  534.9 87.5 reduce-scatter.15
  629.4 224.1 all-reduce.3
where the time goes:
time: 881 us; the launch traced here: 872 us
  waiting for transfers between devices  568 us (64%)
  matrix products  106 us (12%)
  blocking collectives  70.7 us (8%)
  local copies, waits for them, and re-layouts  59.4 us (7%)
  other arithmetic  39 us (4%)
  between operations  16.5 us (2%)
  starting transfers between devices  13 us (1%)
    psum x1, waiting for transfers between devices, shards(): lax.psum((query_weight_grad, key_weight_grad, value_weight_grad, out_weig...  229 us
    reduce_scatter x1, waiting for transfers between devices, shards(): lax.psum_scatter(gate_grad.astype(jnp.bfloat16), 'dp', scatter_dimension=...  89.1 us
    reduce_scatter x1, waiting for transfers between devices, shards(): lax.psum_scatter(up_grad.astype(jnp.bfloat16), 'dp', scatter_dimension=0,...  89.1 us
    psum x1, blocking collectives, shards(): lax.psum((query_weight_grad, key_weight_grad, value_weight_grad, out_weig...  42.1 us
    dot_general x11, matrix products, product_tn(): lax.dot_general(left, right, (((0,), (0,)), ((), ())), preferred_element_...  41.5 us
    dot_general x11, matrix products, product_nt(): lax.dot_general(left, right, (((1,), (1,)), ((), ())), preferred_element_...  33.2 us
    reduce_scatter x1, waiting for transfers between devices, shards(): lax.psum_scatter((product_nt(gate_grad_low, gate_weight) + product_nt(up_...  33 us
    reduce_scatter x1, waiting for transfers between devices, shards(): lax.psum_scatter(product(lax.slice_in_dim(hidden_low, 0, tok_rows * lax.a...  32.9 us
  transfers between devices with their start and end apart: 13, of which 10 were waited for; matrix products, arithmetic and copies ran while one was open for 8% of the time, Pallas kernels for 0%

commit v1 on v0

--- a/solution.py
+++ b/solution.py
@@ -2,12 +2,14 @@
 
 import jax
 import jax.numpy as jnp
+import numpy as np
 from jax import lax
 from jax.sharding import PartitionSpec as P
 
 EPSILON = 1e-06
 ROPE_BASE = 1000000.0
 MASKED = -1e30
+DOC_MOST = 512
 
 
 def for_sending(x):
@@ -85,7 +87,6 @@
     head_dim = key_weight.shape[1]
     query_heads = query_weight.shape[1] // head_dim
     seq_len = segments.shape[1]
-    block_rows = min(512, seq_len)
     score_scale = head_dim ** (-0.5)
     gelu_tanh = partial(jax.nn.gelu, approximate=True)
     x_rows = inputs[0].astype(jnp.float32)
@@ -93,49 +94,44 @@
     all_positions = positions_of(segment_ids)
     own_start = lax.axis_index("head") * tok_rows
     positions = lax.dynamic_slice_in_dim(all_positions, own_start, tok_rows)
-    position_index = jnp.arange(seq_len, dtype=jnp.int32)
     normed, input_pull = jax.vjp(rms_norm, x_rows, input_gain)
     normed_low = normed.astype(low_type)
     q_proj = product(normed_low, query_weight).reshape(tok_rows, query_heads, head_dim)
     k_proj = product(normed_low, key_weight)
     v_low = product(normed_low, value_weight).astype(low_type)
+    k_normed, key_pull = jax.vjp(rms_norm, k_proj, key_gain)
+    k_low = rotary(k_normed, positions, 1.0).astype(low_type)
+    kv_rows = lax.all_gather(
+        jnp.concatenate([k_low, v_low], axis=1), "head", axis=0, tiled=True
+    )
     q_normed, query_pull = jax.vjp(rms_norm, q_proj, query_gain)
-    k_normed, key_pull = jax.vjp(rms_norm, k_proj, key_gain)
     q_low = rotary(q_normed, positions, 1.0).astype(low_type)
-    k_low = rotary(k_normed, positions, 1.0).astype(low_type)
-    query_rows = lax.all_to_all(q_low, "head", split_axis=1, concat_axis=0, tiled=True)[:, 0, :]
-    row_segments_all = jnp.take(segment_ids, position_index)
-    key_rows, value_rows = (
-        lax.all_gather(k_low, "head", axis=0, tiled=True),
-        lax.all_gather(v_low, "head", axis=0, tiled=True),
-    )
-
-    def masked_scores(start_row):
-        row_slice = query_rows[start_row : start_row + block_rows]
-        raw_scores = product_nt(row_slice, key_rows) * score_scale
-        row_ids = position_index[start_row : start_row + block_rows]
-        row_segments = row_segments_all[start_row : start_row + block_rows]
-        allowed = (row_segments[:, None] == segment_ids[None, :]) & (
-            position_index[None, :] <= row_ids[:, None]
-        )
-        return jnp.where(allowed, raw_scores, MASKED)
-
-    attended_blocks = []
-    log_blocks = []
-    for start_row in range(0, seq_len, block_rows):
-        masked = masked_scores(start_row)
-        row_max = jnp.max(masked, axis=1, keepdims=True)
-        exponent = jnp.exp(masked - row_max)
-        row_total = jnp.sum(exponent, axis=1, keepdims=True)
-        probabilities = (exponent / row_total).astype(low_type)
-        attended_blocks.append(product(probabilities, value_rows))
-        log_blocks.append(row_max + jnp.log(row_total))
-    attended_low = jnp.concatenate(attended_blocks, axis=0).astype(low_type)
-    log_totals = jnp.concatenate(log_blocks, axis=0)
-    mixed_rows = lax.all_to_all(
-        attended_low[:, None, :], "head", split_axis=0, concat_axis=1, tiled=True
-    )
-    mixed_rows = mixed_rows.reshape(tok_rows, query_heads * head_dim)
+    query_rows = jnp.concatenate([q_low[:, h, :] for h in range(query_heads)], axis=0)
+    window = min(seq_len, tok_rows + DOC_MOST)
+    window_start = jnp.maximum(own_start + tok_rows - window, 0)
+    kv_window = lax.dynamic_slice_in_dim(kv_rows, window_start, window)
+    key_rows = kv_window[:, :head_dim]
+    value_rows = kv_window[:, head_dim:]
+    own_segments = lax.dynamic_slice_in_dim(segment_ids, own_start, tok_rows)
+    key_segments = lax.dynamic_slice_in_dim(segment_ids, window_start, window)
+    own_index = own_start + jnp.arange(tok_rows, dtype=jnp.int32)
+    key_index = window_start + jnp.arange(window, dtype=jnp.int32)
+    allowed = (own_segments[:, None] == key_segments[None, :]) & (
+        key_index[None, :] <= own_index[:, None]
+    )
+    raw_scores = product_nt(query_rows, key_rows) * score_scale
+    masked = jnp.where(
+        allowed[None], raw_scores.reshape(query_heads, tok_rows, window), MASKED
+    ).reshape(query_heads * tok_rows, window)
+    row_max = jnp.max(masked, axis=1, keepdims=True)
+    exponent = jnp.exp(masked - row_max)
+    row_total = jnp.sum(exponent, axis=1, keepdims=True)
+    probabilities = exponent / row_total
+    probs_low = probabilities.astype(low_type)
+    attended_low = product(probs_low, value_rows).astype(low_type)
+    mixed_rows = jnp.concatenate(
+        [attended_low[h * tok_rows : (h + 1) * tok_rows] for h in range(query_heads)], axis=1
+    )
     projected = product(mixed_rows, out_weight)
     attn_branch, attn_pull = jax.vjp(rms_norm, projected, attn_gain)
     after_attn = x_rows + attn_branch
@@ -179,37 +175,28 @@
     projected_low = projected_grad.astype(low_type)
     out_weight_grad = product_tn(mixed_rows, projected_low)
     mixed_grad = product_nt(projected_low, out_weight).astype(low_type)
-    mixed_grad = mixed_grad.reshape(tok_rows, query_heads, head_dim)
-    attended_grad = lax.all_to_all(mixed_grad, "head", split_axis=1, concat_axis=0, tiled=True)[
-        :, 0, :
-    ]
-    query_blocks = []
-    key_grad = jnp.zeros((seq_len, head_dim), jnp.float32)
-    value_grad = jnp.zeros((seq_len, head_dim), jnp.float32)
-    for start_row in range(0, seq_len, block_rows):
-        masked = masked_scores(start_row)
-        probabilities = jnp.exp(masked - log_totals[start_row : start_row + block_rows])
-        grad_rows = attended_grad[start_row : start_row + block_rows]
-        value_grad = value_grad + product_tn(probabilities.astype(low_type), grad_rows)
-        prob_grad = product_nt(grad_rows, value_rows)
-        row_delta = jnp.sum(prob_grad * probabilities, axis=1, keepdims=True)
-        score_grad = (probabilities * (prob_grad - row_delta)).astype(low_type)
-        query_blocks.append(product(score_grad, key_rows) * score_scale)
-        key_grad = (
-            key_grad
-            + product_tn(score_grad, query_rows[start_row : start_row + block_rows]) * score_scale
-        )
-    query_grad_low = jnp.concatenate(query_blocks, axis=0).astype(low_type)
-    query_back = lax.all_to_all(
-        query_grad_low[:, None, :], "head", split_axis=0, concat_axis=1, tiled=True
-    )
-    key_share, value_share = (
-        lax.psum_scatter(
-            key_grad.astype(jnp.bfloat16), "head", scatter_dimension=0, tiled=True
-        ).astype(jnp.float32),
-        lax.psum_scatter(
-            value_grad.astype(jnp.bfloat16), "head", scatter_dimension=0, tiled=True
-        ).astype(jnp.float32),
+    attended_grad = jnp.concatenate(
+        [mixed_grad[:, h * head_dim : (h + 1) * head_dim] for h in range(query_heads)], axis=0
+    )
+    value_grad = product_tn(probs_low, attended_grad)
+    prob_grad = product_nt(attended_grad, value_rows)
+    row_delta = jnp.sum(prob_grad * probabilities, axis=1, keepdims=True)
+    score_grad = (probabilities * (prob_grad - row_delta)).astype(low_type)
+    query_grad_low = (product(score_grad, key_rows) * score_scale).astype(low_type)
+    key_grad = product_tn(score_grad, query_rows) * score_scale
+    kv_grad = lax.dynamic_update_slice_in_dim(
+        jnp.zeros((seq_len, 2 * head_dim), low_type),
+        jnp.concatenate([key_grad, value_grad], axis=1).astype(low_type),
+        window_start,
+        axis=0,
+    )
+    kv_share = lax.psum_scatter(kv_grad, "head", scatter_dimension=0, tiled=True).astype(
+        jnp.float32
+    )
+    key_share = kv_share[:, :head_dim]
+    value_share = kv_share[:, head_dim:]
+    query_back = jnp.stack(
+        [query_grad_low[h * tok_rows : (h + 1) * tok_rows] for h in range(query_heads)], axis=1
     )
     q_proj_grad, query_gain_grad = query_pull(
         rotary(query_back.astype(jnp.float32), positions, -1.0)
@@ -229,20 +216,20 @@
     )
     input_from_norm, input_gain_grad = input_pull(normed_grad)
     input_grad = after_grad + input_from_norm
-    summed = lax.psum(
-        (
-            query_weight_grad,
-            key_weight_grad,
-            value_weight_grad,
-            out_weight_grad,
-            input_gain_grad,
-            query_gain_grad,
-            key_gain_grad,
-            attn_gain_grad,
-            pre_gain_grad,
-            post_gain_grad,
-        ),
-        ("dp", "head"),
+    weight_grads = (query_weight_grad, key_weight_grad, value_weight_grad, out_weight_grad)
+    gain_grads = (
+        input_gain_grad,
+        query_gain_grad,
+        key_gain_grad,
+        attn_gain_grad,
+        pre_gain_grad,
+        post_gain_grad,
+    )
+    gain_sums = lax.psum(jnp.concatenate(gain_grads), ("dp", "head"))
+    gain_ends = np.cumsum([g.shape[0] for g in gain_grads])
+    weight_sums = lax.psum(tuple(w.astype(low_type) for w in weight_grads), ("dp", "head"))
+    summed = tuple(w.astype(jnp.float32) for w in weight_sums) + tuple(
+        gain_sums[end - g.shape[0] : end] for g, end in zip(gain_grads, gain_ends)
     )
     gate_share, up_share, down_share = (
         lax.psum_scatter(

time: 881 us -> 725 us (0.82)
  waiting for transfers between devices: 568 us -> 488 us
  local copies, waits for them, and re-layouts: 59.4 us -> 28.5 us
  blocking collectives: 70.7 us -> 41.2 us
  starting transfers between devices: 13 us -> 1.52 us
    psum x1, waiting for transfers between devices: 229 us -> 158 us  [shards(): lax.psum(tuple((w.astype(low_type) for w in weight_grads)), ('dp', 'head'))]
    unnamed x205 -> x202, local copies, waits for them, and re-layouts: 32.8 us -> 13.9 us
    all_to_all x3 -> x0, waiting for transfers between devices: 16.7 us -> none  [the longest x1 8.76 us: shards(): lax.all_to_all(mixed_grad, 'head', split_axis=1, concat_axis=0, tiled=True)]
    all_gather x2 -> x0, blocking collectives: 16.3 us -> none  [the longest x1 9.05 us: shards(): lax.all_gather(k_low, 'head', axis=0, tiled=True)]
    all_to_all x1 -> x0, blocking collectives: 12.3 us -> none  [shards(): lax.all_to_all(attended_low[:, None, :], 'head', split_axis=0, concat_axi...]
    all_to_all x3 -> x0, starting transfers between devices: 12 us -> none  [the longest x1 4.29 us: shards(): lax.all_to_all(mixed_grad, 'head', split_axis=1, concat_axis=0, tiled=True)]
    convert_element_type x0 -> x5, other arithmetic: none -> 9.53 us  [the longest x4 9.44 us: shards(): w.astype(jnp.float32)]
    gather x1 -> x0, local copies, waits for them, and re-layouts: 9.08 us -> none  [shards(): row_segments_all = jnp.take(segment_ids, position_index)]
  transfers between devices with their start and end apart: 13 -> 10, of which waited for: 10 -> 9; matrix products, arithmetic and copies ran while one was open for 8% -> 8% of each run, Pallas kernels for 0% -> 0%
where the time goes in v1:
time: 725 us; the launch traced here: 717 us
  waiting for transfers between devices  488 us (67%)
  matrix products  100 us (14%)
  blocking collectives  41.2 us (6%)
  other arithmetic  41 us (6%)
  local copies, waits for them, and re-layouts  28.5 us (4%)
  between operations  16.5 us (2%)
    psum x1, waiting for transfers between devices, shards(): lax.psum(tuple((w.astype(low_type) for w in weight_grads)), ('dp', 'head'))  158 us
    reduce_scatter x1, waiting for transfers between devices, shards(): lax.psum_scatter(up_grad.astype(jnp.bfloat16), 'dp', scatter_dimension=0,...  89.7 us
    reduce_scatter x1, waiting for transfers between devices, shards(): lax.psum_scatter(gate_grad.astype(jnp.bfloat16), 'dp', scatter_dimension=...  89.7 us
    psum x1, blocking collectives, shards(): gain_sums = lax.psum(jnp.concatenate(gain_grads), ('dp', 'head'))  41.2 us
    dot_general x9, matrix products, product_tn(): lax.dot_general(left, right, (((0,), (0,)), ((), ())), preferred_element_...  34.2 us
    dot_general x9, matrix products, product_nt(): lax.dot_general(left, right, (((1,), (1,)), ((), ())), preferred_element_...  34.1 us
    reduce_scatter x1, waiting for transfers between devices, shards(): lax.psum_scatter(product(lax.slice_in_dim(hidden_low, 0, tok_rows * lax.a...  32.9 us
    reduce_scatter x1, waiting for transfers between devices, shards(): lax.psum_scatter((product_nt(gate_grad_low, gate_weight) + product_nt(up_...  32.7 us
  transfers between devices with their start and end apart: 10, of which 9 were waited for; matrix products, arithmetic and copies ran while one was open for 8% of the time, Pallas kernels for 0%

profile of v1, /device:TPU:0, one launch (start us, length us, event | category | flops | bytes accessed | tf_op | source)
XLA Modules:
  0.0 717.4 jit_solution(9379533610855343231)
XLA Ops:
  7.3 1.4 fusion.28
  8.8 1.8 multiply_reduce_fusion.10
  12.4 2.2 convolution_convert_fusion.11
  15.4 1.7 pad_maximum_fusion.5
  17.2 4.3 copy.33
  22.6 1.3 copy.34
  23.9 2.6 multiply_reduce_fusion.7
  28.6 8.3 %all-gather.4.cloned.1.call-done = bf16[1024,512]{0,1:T(8,128)(2,1)} async-done(((bf16[256,512]{0,1:T(8,128)(2,1)}), bf16[1024,512]{0,1:T(8,128)(2,1)}) %all-gather.4.cloned.1.call-update) | async-done | bytes 1048592 | tf_op jit(solution)/shard_map/all_gather | solution.py:104
  36.8 2.1 fusion.104
  39.5 2.3 convolution_convert_fusion.9
  46.6 23.7 %all-gather.6.cloned.1.call-done = bf16[1024,1152]{1,0:T(8,128)(2,1)} async-done(((bf16[256,1152]{1,0:T(8,128)(2,1)}), bf16[1024,1152]{1,0:T(8,128)(2,1)}) %all-gather.6.cloned.1.call-update) | async-done | bytes 2359312 | tf_op jit(solution)/shard_map/all_gather | solution.py:139
  70.3 7.4 %fusion.105 = f32[1024,1728]{0,1:T(8,128)S(1)} fusion(bf16[1024,1152]{1,0:T(8,128)(2,1)} %all-gather.6.cloned.1.call-done, bf16[1152,1728]{0,1:T(8,128)(2,1)} %param.23), kind=kOutput, calls=%fused_computation.207 | convolution fusion | flops 4076863488 | bytes 13418496 | tf_op jit(solution)/shard_map/dot_general | solution.py:52
  77.7 7.9 %multiply_convert_fusion.1 = (bf16[1024,1728]{0,1:T(8,128)(2,1)S(1)}, f32[1024,1728]{0,1:T(8,128)}) fusion(f32[1024,1728]{0,1:T(8,128)S(1)} %fusion.105, bf16[1024,1152]{1,0:T(8,128)(2,1)S(1)} %copy-done.91, bf16[1152,1728]{0,1:T(8,128)(2,1)S(1)} %copy-done.89), kind=kOutput, calls=%fused_computation.13 | convolution fusion | flops 4094558208 | bytes 24035328 | tf_op jit(solution)/shard_map/dot_general | solution.py:52
  85.6 1.8 copy-done.95
  87.4 6.3 convolution_convert_fusion.5
  93.8 32.9 %reduce-scatter.7.cloned.1.call-done = bf16[256,1152]{1,0:T(8,128)(2,1)} async-done(((bf16[1024,1152]{1,0:T(8,128)(2,1)}), bf16[256,1152]{1,0:T(8,128)(2,1)}) %reduce-scatter.7.cloned.1.call-update) | async-done | bytes 589840 | tf_op jit(solution)/shard_map/reduce_scatter | solution.py:144
  126.7 1.3 fusion.37
  128.0 2.4 fusion.36
  130.4 2.4 fusion.32
  133.0 24.0 %all-gather.8.cloned.1.call-done = bf16[1024,1152]{1,0:T(8,128)(2,1)} async-done(((bf16[256,1152]{1,0:T(8,128)(2,1)}), bf16[1024,1152]{1,0:T(8,128)(2,1)}) %all-gather.8.cloned.1.call-update) | async-done | bytes 2359312 | tf_op jit(solution)/shard_map/all_gather | solution.py:156
  157.0 14.8 %multiply_convert_fusion = (bf16[1024,1728]{0,1:T(8,128)(2,1)S(1)}, bf16[1024,1728]{0,1:T(8,128)(2,1)S(1)}) fusion(f32[1024,1728]{0,1:T(8,128)} %copy-done.96, f32[1024,1728]{0,1:T(8,128)} %get-tuple-element.81, bf16[1024,1152]{1,0:T(8,128)(2,1)} %all-gather.8.cloned.1.call-done, bf16[1728,1152]{1,0:T(8,128)(2,1)} %param.25), kind=kOutput, calls=%fused_computation.12 | convolution fusion | flops 4119330816 | bytes 27574272 | tf_op jit(solution)/shard_map/dot_general | solution.py:62
  171.9 5.2 fusion.106
  177.1 6.5 add_convert_fusion
  183.8 32.7 %reduce-scatter.9.cloned.1.call-done = bf16[256,1152]{1,0:T(8,128)(2,1)} async-done(((bf16[1024,1152]{1,0:T(8,128)(2,1)}), bf16[256,1152]{1,0:T(8,128)(2,1)}) %reduce-scatter.9.cloned.1.call-update) | async-done | bytes 589840 | tf_op jit(solution)/shard_map/reduce_scatter | solution.py:164
  216.6 2.1 fusion.27
  219.4 3.9 multiply_reduce_fusion.1
  231.0 7.3 %dynamic_update_slice.3 = bf16[1024,512]{0,1:T(8,128)(2,1)S(1)} dynamic-update-slice(bf16[1024,512]{0,1:T(8,128)(2,1)S(1)} %broadcast_in_dim.45, bf16[768,512]{0,1:T(8,128)(2,1)S(1)} %pad_maximum_fusion.1, s32[]{:T(128)S(6)} %max.3, s32[]{:T(128)} %constant.26.clone.1) | dynamic-update-slice | bytes 1572868 | tf_op jit(solution)/shard_map/dynamic_update_slice | solution.py:187
  239.3 9.2 %convolution_convert_fusion = bf16[1728,1152]{0,1:T(8,128)(2,1)} fusion(bf16[1024,1728]{0,1:T(8,128)(2,1)} %copy-done.95, bf16[1024,1152]{1,0:T(8,128)(2,1)} %all-gather.8.cloned.1.call-done), kind=kOutput, calls=%fused_computation.2 | convolution fusion | flops 4078854144 | bytes 9879552 | tf_op jit(solution)/shard_map/dot_general | solution.py:56
  248.8 1.3 copy-done.92
  250.2 8.1 %convolution_convert_fusion.2 = bf16[1152,1728]{1,0:T(8,128)(2,1)} fusion(bf16[1024,1152]{1,0:T(8,128)(2,1)S(1)} %copy-done.92, bf16[1024,1728]{0,1:T(8,128)(2,1)} %copy-done.94), kind=kOutput, calls=%fused_computation.4 | convolution fusion | flops 4078854144 | bytes 9879552 | tf_op jit(solution)/shard_map/dot_general | solution.py:56
  258.4 8.1 %convolution_convert_fusion.1 = bf16[1152,1728]{1,0:T(8,128)(2,1)} fusion(bf16[1024,1152]{1,0:T(8,128)(2,1)S(1)} %copy-done.92, bf16[1024,1728]{0,1:T(8,128)(2,1)} %copy-done.97), kind=kOutput, calls=%fused_computation.3 | convolution fusion | flops 4078854144 | bytes 9879552 | tf_op jit(solution)/shard_map/dot_general | solution.py:56
  266.6 1.3 copy-done.19
  269.0 2.3 convolution_convert_fusion.3
  274.3 1.3 convolution_convert_fusion.7
  275.6 1.3 convolution_convert_fusion.6
  277.1 2.4 convolution_convert_fusion.4
  279.6 2.6 fusion.107
  284.1 41.2 %psum.39 = f32[5120]{0:T(1024)S(1)} all-reduce(f32[5120]{0:T(1024)S(1)} %constant_dynamic-update-slice_fusion), channel_id=1, replica_groups=mesh['dp'=8,'head'=4] {'dp','head'}, use_global_device_ids=true, to_apply=%region_33.34 | all-reduce | flops 5120 | bytes 40960 | tf_op jit(solution)/shard_map/psum | solution.py:228
  326.5 1.3 fusion.35
  327.9 29.2 %reduce-scatter.17.cloned.1.call-done = bf16[1728,144]{0,1:T(8,128)(2,1)} async-done(((bf16[1728,1152]{0,1:T(8,128)(2,1)}), bf16[1728,144]{0,1:T(8,128)(2,1)}) %reduce-scatter.17.cloned.1.call-update) | async-done | bytes 497680 | tf_op jit(solution)/shard_map/reduce_scatter | solution.py:241
  357.1 2.1 convert_element_type.190
  359.1 89.7 %reduce-scatter.13.cloned.1.call-done = bf16[144,1728]{1,0:T(8,128)(2,1)} async-done(((bf16[1152,1728]{1,0:T(8,128)(2,1)}), bf16[144,1728]{1,0:T(8,128)(2,1)}) %reduce-scatter.13.cloned.1.call-update) | async-done | bytes 497680 | tf_op jit(solution)/shard_map/reduce_scatter | solution.py:235
  448.8 2.1 convert_element_type.186
  450.9 89.7 %reduce-scatter.15.cloned.1.call-done = bf16[144,1728]{1,0:T(8,128)(2,1)} async-done(((bf16[1152,1728]{1,0:T(8,128)(2,1)}), bf16[144,1728]{1,0:T(8,128)(2,1)}) %reduce-scatter.15.cloned.1.call-update) | async-done | bytes 497680 | tf_op jit(solution)/shard_map/reduce_scatter | solution.py:238
  540.5 2.1 convert_element_type.188
  542.6 158.0 %all-reduce.3.cloned.1.call-done = (bf16[1152,1024]{1,0:T(8,128)(2,1)}, bf16[1152,256]{1,0:T(8,128)(2,1)}, bf16[1152,256]{1,0:T(8,128)(2,1)}, bf16[1024,1152]{1,0:T(8,128)(2,1)}) async-done(((bf16[1152,1024]{1,0:T(8,128)(2,1)}, bf16[1152,256]{1,0:T(8,128)(2,1)}, bf16[1152,256]{1,0:T(8,128)(2,1)}, bf16[1024,1152]{1,0:T(8,128)(2,1)}), (bf16[1152,1024]{1,0:T(8,128)(2,1)}, bf16[1152,256]{1,0:T(8,128)(2,1)}, ...) | async-done | bytes 5898256 | tf_op jit(solution)/shard_map/psum | solution.py:230
  700.6 4.5 convert_element_type.178
  705.2 2.7 convert_element_type.184
  (283 shorter events, 30.0 us)
Async XLA Ops:
  7.2 34.7 %copy-start = (bf16[1024,1152]{1,0:T(8,128)(2,1)S(1)}, bf16[1024,1152]{1,0:T(8,128)(2,1)}, u32[]{:S(2)}) copy-start(bf16[1024,1152]{1,0:T(8,128)(2,1)} %param.22) | copy-start | bytes 7077892
  7.2 5.2 copy-start.2
  7.2 5.2 copy-start.50
  7.2 7.5 %copy-start.75 = (f32[256]{0:T(256)S(1)}, f32[256]{0:T(256)}, u32[]{:S(2)}) copy-start(f32[256]{0:T(256)} %param.28) | copy-start | bytes 3076
  7.2 29.6 %all-gather.4.cloned.1.call-start = ((), (), s32[]{:S(2)}) async-start(), calls=%async_computation.6 | async-start | bytes 1310720 | tf_op jit(solution)/shard_map/all_gather | solution.py:104
  7.3 8.1 %copy-start.85 = (f32[128]{0:T(128)}, f32[128]{0:T(128)S(1)}, u32[]{:S(2)}) copy-start(f32[128]{0:T(128)S(1)} %multiply_power_fusion) | copy-start | bytes 1540
  8.7 6.0 copy-start.79
  8.7 15.1 %copy-start.58 = (f32[256]{0:T(256)}, f32[256]{0:T(256)S(1)}, u32[]{:S(2)}) copy-start(f32[256]{0:T(256)S(1)} %fusion.81) | copy-start | bytes 3076
  10.5 11.0 %copy-start.15 = (f32[256,256]{0,1:T(8,128)}, f32[256,256]{0,1:T(8,128)S(1)}, u32[]{:S(2)}) copy-start(f32[256,256]{0,1:T(8,128)S(1)} %get-tuple-element.73) | copy-start | bytes 786436
  10.6 4.2 copy-start.64
  15.4 12.3 %copy-start.20 = (f32[256,128]{0,1:T(8,128)}, f32[256,128]{0,1:T(8,128)S(1)}, u32[]{:S(2)}) copy-start(f32[256,128]{0,1:T(8,128)S(1)} %get-tuple-element.68) | copy-start | bytes 393220
  17.1 53.1 %all-gather.6.cloned.1.call-start = ((), (), s32[]{:S(2)}) async-start(), calls=%async_computation.7 | async-start | bytes 2949120 | tf_op jit(solution)/shard_map/all_gather | solution.py:139
  23.9 3.6 copy-start.72
  27.5 9.3 %copy-start.22 = (pred[96,8,4,256]{3,1,2,0:T(8,128)(4,1)S(1)}, pred[96,8,4,256]{3,1,2,0:T(8,128)(4,1)}, u32[]{:S(2)}) copy-start(pred[96,8,4,256]{3,1,2,0:T(8,128)(4,1)} %copy.34) | copy-start | bytes 2359300
  28.6 10.4 %copy-start.39 = (bf16[256,256]{0,1:T(8,128)(2,1)}, bf16[256,256]{0,1:T(8,128)(2,1)S(1)}, u32[]{:S(2)}) copy-start(bf16[256,256]{0,1:T(8,128)(2,1)S(1)} %get-tuple-element.53) | copy-start | bytes 393220
  28.6 10.4 %copy-start.41 = (bf16[256,256]{0,1:T(8,128)(2,1)}, bf16[256,256]{0,1:T(8,128)(2,1)S(1)}, u32[]{:S(2)}) copy-start(bf16[256,256]{0,1:T(8,128)(2,1)S(1)} %get-tuple-element.54) | copy-start | bytes 393220
  28.6 10.4 %copy-start.43 = (bf16[256,256]{0,1:T(8,128)(2,1)}, bf16[256,256]{0,1:T(8,128)(2,1)S(1)}, u32[]{:S(2)}) copy-start(bf16[256,256]{0,1:T(8,128)(2,1)S(1)} %get-tuple-element.55) | copy-start | bytes 393220
  46.1 80.7 %reduce-scatter.7.cloned.1.call-start = ((), (), s32[]{:S(2)}) async-start(), calls=%async_computation.8 | async-start | bytes 2949120 | tf_op jit(solution)/shard_map/reduce_scatter | solution.py:144
  70.3 7.4 %copy-start.89 = (bf16[1152,1728]{0,1:T(8,128)(2,1)S(1)}, bf16[1152,1728]{0,1:T(8,128)(2,1)}, u32[]{:S(2)}) copy-start(bf16[1152,1728]{0,1:T(8,128)(2,1)} %param.24) | copy-start | bytes 11943940
  70.3 7.4 %copy-start.91 = (bf16[1024,1152]{1,0:T(8,128)(2,1)S(1)}, bf16[1024,1152]{1,0:T(8,128)(2,1)}, u32[]{:S(2)}) copy-start(bf16[1024,1152]{1,0:T(8,128)(2,1)} %all-gather.6.cloned.1.call-done) | copy-start | bytes 7077892
  77.7 7.9 %copy-start.96 = (f32[1024,1728]{0,1:T(8,128)}, f32[1024,1728]{0,1:T(8,128)S(1)}, u32[]{:S(2)}) copy-start(f32[1024,1728]{0,1:T(8,128)S(1)} %fusion.105) | copy-start | bytes 21233668
  77.7 9.7 %copy-start.87 = (bf16[1728,1152]{1,0:T(8,128)(2,1)S(1)}, bf16[1728,1152]{1,0:T(8,128)(2,1)}, u32[]{:S(2)}) copy-start(bf16[1728,1152]{1,0:T(8,128)(2,1)} %param.25) | copy-start | bytes 11943940
  93.7 34.3 %copy-start.47 = (f32[1152]{0:T(1024)S(1)}, f32[1152]{0:T(1024)}, u32[]{:S(2)}) copy-start(f32[1152]{0:T(1024)} %param.31) | copy-start | bytes 13828
  93.8 63.2 %all-gather.8.cloned.1.call-start = ((), (), s32[]{:S(2)}) async-start(), calls=%async_computation.9 | async-start | bytes 2949120 | tf_op jit(solution)/shard_map/all_gather | solution.py:156
  132.8 83.7 %reduce-scatter.9.cloned.1.call-start = ((), (), s32[]{:S(2)}) async-start(), calls=%async_computation.10 | async-start | bytes 2949120 | tf_op jit(solution)/shard_map/reduce_scatter | solution.py:164
  157.0 14.9 %copy-start.88 = (bf16[1152,1728]{0,1:T(8,128)(2,1)S(1)}, bf16[1152,1728]{0,1:T(8,128)(2,1)}, u32[]{:S(2)}) copy-start(bf16[1152,1728]{0,1:T(8,128)(2,1)} %param.23) | copy-start | bytes 11943940
  171.9 5.2 copy-start.94
  171.9 5.2 copy-start.97
  171.9 5.2 copy-start.90
  183.6 87.7 %reduce-scatter.11.cloned.1.call-start = ((), (), s32[]{:S(2)}) async-start(), calls=%async_computation.11 | async-start | bytes 1310720 | tf_op jit(solution)/shard_map/reduce_scatter | solution.py:193
  219.4 3.9 copy-start.84
  219.4 3.9 copy-start.49
  219.4 3.9 copy-start.67
  239.3 117.8 %reduce-scatter.17.cloned.1.call-start = ((), (), s32[]{:S(2)}) async-start(), calls=%async_computation.14 | async-start | bytes 4644864 | tf_op jit(solution)/shard_map/reduce_scatter | solution.py:241
  248.5 200.2 %reduce-scatter.13.cloned.1.call-start = ((), (), s32[]{:S(2)}) async-start(), calls=%async_computation.12 | async-start | bytes 4644864 | tf_op jit(solution)/shard_map/reduce_scatter | solution.py:235
  258.3 282.2 %reduce-scatter.15.cloned.1.call-start = ((), (), s32[]{:S(2)}) async-start(), calls=%async_computation.13 | async-start | bytes 4644864 | tf_op jit(solution)/shard_map/reduce_scatter | solution.py:238
  266.6 434.1 %all-reduce.3.cloned.1.call-start = ((), (), s32[]{:S(2)}) async-start(), calls=%async_computation.15 | async-start | bytes 11796480 | tf_op jit(solution)/shard_map/psum | solution.py:230
  269.0 3.4 copy-start.78
  269.0 3.4 copy-start.86
  269.0 3.9 copy-start.16
  269.0 3.9 copy-start.65
  269.0 3.9 copy-start.76
  269.0 4.1 copy-start.21
  283.3 42.0 %copy-start.80 = (f32[256]{0:T(256)S(1)}, f32[256]{0:T(256)}, u32[]{:S(2)}) copy-start(f32[256]{0:T(256)} %copy-done.79) | copy-start | bytes 3076
  283.3 43.2 %copy-start.8 = (f32[256,1152]{1,0:T(8,128)S(1)}, f32[256,1152]{1,0:T(8,128)}, u32[]{:S(2)}) copy-start(f32[256,1152]{1,0:T(8,128)} %copy-done.7) | copy-start | bytes 3538948
  700.6 4.5 copy-start.14
  705.2 3.8 copy-start.26
  705.2 4.9 copy-start.1
  (60 other events, 91.2 us)
Sparse Core Ops, SparseCore 0:
  17.3 19.5 all-gather.3
  46.2 24.0 all-gather.5
  93.9 32.8 reduce-scatter.6
  132.9 24.0 all-gather.7
  183.7 32.8 reduce-scatter.8
  239.4 24.7 reduce-scatter.10
  267.8 89.2 reduce-scatter.16
  361.2 87.5 reduce-scatter.12
  452.9 87.5 reduce-scatter.14
  547.2 153.4 all-reduce.2
